TPU v7x, 256 devices: a whole 4x4x8 slice. The times are simulated.
256 devices in a mesh: grp: 8 (over x, core), vocab: 32 (over y, z).
Axes of the slice: x: 4, y: 4, z: 8, core: 2. Of those that a mesh axis runs over, the one named last changes fastest.
Arguments:
- hidden: bfloat16 [1024, 16384], P('grp', 'vocab'), may hold values from -6 to 6
- flags: int32 [1024, 1], P('grp'), may hold values from 0 to 8; in each aligned block of 128 rows (0 to 127, 128 to 255, ...) at most 16 rows name the same one
- targets: int32 [1024], P('grp'), may hold values from 0 to 65535
- head: bfloat16 [16384, 65536], P('grp', 'vocab'), may hold values from -0.140625 to 0.140625
- lengths: int32 [8, 8], P('grp'), may hold values from 1 to 64, 128 in all within a row
Outputs:
- token_scores: float32 [1024], P('grp')
- doc_scores: float32 [8, 8], P('grp')
Inputs may be any that keep to these rules, and one draw needn't show every extreme that they name: `flags`: A value below 8 names the scorer group of a scored row. Within the 128 rows of one shard no value occurs more than 16 times, and in every draw some value occurs exactly 16 times in some shard.
All inputs are finite; a program needn't handle non-finite values.
Results may differ from a plain program's by a relative error of at most 0.0003.
Values may be sent and summed in bfloat16 or wider, within the bound.
A program may use at most 128 MiB of HBM per device.

v0:
```python
import jax
import jax.numpy as jnp
from jax import lax
from jax.sharding import PartitionSpec as P


def combined_all(part, axis, combine):
    gathered = jax.tree.map(lambda a: lax.all_gather(a, axis), part)

    def take(source):
        return jax.tree.map(lambda a: lax.dynamic_index_in_dim(a, source, 0, False), gathered)

    return lax.fori_loop(
        1, lax.axis_size(axis), lambda source, state: combine(state, take(source)), take(0)
    )


def slot_table(flag_col, groups, capacity, shard_rows):
    values = jnp.arange(groups + 1, dtype=jnp.int32)
    onehot = (flag_col[:, None] == values[None, :]).astype(jnp.int32)
    ranking = jnp.sum((jnp.cumsum(onehot, axis=0) - 1) * onehot, axis=1)
    where_to = jnp.where(flag_col < groups, flag_col * capacity + ranking, groups * capacity)
    table = jnp.full((groups * capacity + 1,), -1, jnp.int32)
    table = table.at[where_to].set(jnp.arange(shard_rows, dtype=jnp.int32))
    return table[: groups * capacity]


def combine_stats(left, right):
    row_max = jnp.maximum(left[0], right[0])
    left_gap = left[0] - row_max
    right_gap = right[0] - row_max
    left_fac = jnp.exp(left_gap)
    right_fac = jnp.exp(right_gap)
    row_total = left_fac * left[1] + right_fac * right[1]
    first_mom = left_fac * (left[2] + left_gap * left[1]) + right_fac * (
        right[2] + right_gap * right[1]
    )
    second_mom = left_fac * (left[3] + 2.0 * left_gap * left[2] + left_gap * left_gap * left[1])
    second_mom = second_mom + right_fac * (
        right[3] + 2.0 * right_gap * right[2] + right_gap * right_gap * right[1]
    )
    return (row_max, row_total, first_mom, second_mom)


def local_stats(logits, target_ids, columns, axis):
    row_max = jnp.max(logits, axis=axis)
    shifted = logits - jnp.expand_dims(row_max, axis)
    scaled = jnp.exp(shifted)
    row_total = jnp.sum(scaled, axis=axis)
    first_mom = jnp.sum(scaled * shifted, axis=axis)
    second_mom = jnp.sum(scaled * shifted * shifted, axis=axis)
    is_target = target_ids[:, None] == columns[None, :]
    target_val = jnp.sum(jnp.where(is_target, logits, jnp.float32(0.0)), axis=axis)
    return (row_max, row_total, first_mom, second_mom, target_val)


def final_scores(target_ids, row_max, row_total, first_mom, second_mom, target_val):
    mean_shift = first_mom / row_total
    row_var = second_mom / row_total - mean_shift * mean_shift
    return jnp.where(
        target_ids >= 0,
        (target_val - row_max - mean_shift) / jnp.sqrt(jnp.maximum(row_var, 1.0)),
        jnp.float32(0.0),
    )


def shards(hidden, flags, targets, head, lengths):
    groups = lax.axis_size("grp")
    shard_rows = hidden.shape[0]
    capacity = shard_rows // groups
    vocab_dev = head.shape[1]
    my_vocab = lax.axis_index("vocab")
    flag_col = flags[:, 0]
    table = slot_table(flag_col, groups, capacity, shard_rows)
    is_live = table >= 0
    safe_rows = jnp.maximum(table, 0)
    pieces = jnp.where(is_live[:, None], hidden[safe_rows], jnp.zeros((), jnp.bfloat16))
    slot_targets = jnp.where(is_live, targets[safe_rows], -1)
    arrived = lax.all_to_all(
        pieces.reshape(groups, capacity, pieces.shape[1]),
        "grp",
        split_axis=0,
        concat_axis=0,
        tiled=True,
    )
    full_rows = lax.all_gather(
        arrived.reshape(shard_rows, pieces.shape[1]), "vocab", axis=1, tiled=True
    )
    block_rows = lax.all_to_all(full_rows, "grp", split_axis=1, concat_axis=0, tiled=True)
    target_ids = lax.all_to_all(
        slot_targets.reshape(groups, capacity), "grp", split_axis=0, concat_axis=0, tiled=True
    ).reshape(shard_rows)
    logits = lax.psum_scatter(
        jnp.dot(block_rows, head, preferred_element_type=jnp.float32),
        "grp",
        scatter_dimension=0,
        tiled=True,
    )
    columns = my_vocab * vocab_dev + jnp.arange(vocab_dev, dtype=jnp.int32)
    row_max, row_total, first_mom, second_mom, target_val = local_stats(
        logits, target_ids, columns, 1
    )
    row_max, row_total, first_mom, second_mom = combined_all(
        (row_max, row_total, first_mom, second_mom), "vocab", combine_stats
    )
    target_val = lax.psum(target_val, "vocab")
    token_scores = final_scores(target_ids, row_max, row_total, first_mom, second_mom, target_val)
    returned = lax.all_to_all(
        token_scores.reshape(groups, capacity), "grp", split_axis=0, concat_axis=0, tiled=True
    ).reshape(shard_rows)
    row_val = (
        jnp.zeros((shard_rows + 1,), jnp.float32)
        .at[jnp.where(is_live, table, shard_rows)]
        .set(returned)[:shard_rows]
    )
    flagged = (flag_col < groups).astype(jnp.float32)
    doc_ends = jnp.cumsum(lengths[0])
    doc_starts = doc_ends - lengths[0]
    positions = jnp.arange(shard_rows, dtype=jnp.int32)
    membership = (
        (positions[None, :] >= doc_starts[:, None]) & (positions[None, :] < doc_ends[:, None])
    ).astype(jnp.float32)
    sums = jnp.sum(membership * row_val[None, :], axis=1)
    counts = jnp.sum(membership * flagged[None, :], axis=1)
    doc_means = (sums / jnp.maximum(counts, 1.0))[None, :]
    return (token_scores, doc_means)


def solution(mesh):
    placed = (P("grp", "vocab"), P("grp", None), P("grp"), P("grp", "vocab"), P("grp", None))
    return jax.shard_map(
        shards, mesh=mesh, in_specs=placed, out_specs=(P("grp"), P("grp", None)), check_vma=False
    )
```

profile of v0, /device:TPU:1, one launch (start us, length us, event | category | flops | bytes accessed | tf_op | source)
XLA Modules:
  0.0 488.9 jit_solution(7191298796290074408)
XLA Ops:
  7.2 0.8 fusion.12
  8.2 0.8 select_reduce_fusion.1
  9.0 0.7 fusion.19
  9.7 1.0 scatter_custom_fusion
  10.8 0.9 gather_fusion.1
  11.7 11.6 %all_to_all.39 = bf16[8,16,512]{2,1,0:T(8,128)(2,1)} all-to-all(bf16[8,16,512]{2,1,0:T(8,128)(2,1)S(1)} %broadcast_select_fusion), channel_id=1, replica_groups=mesh['grp'=8,'vocab'=32] {'grp'}, dimensions={0} | all-to-all | bytes 262144 | tf_op jit(solution)/shard_map/all_to_all | solution.py:79
  23.4 80.8 %all-gather.10.cloned.1.call-done = bf16[128,16384]{1,0:T(8,128)(2,1)} async-done(((bf16[128,512]{1,0:T(8,128)(2,1)}), bf16[128,16384]{1,0:T(8,128)(2,1)}) %all-gather.10.cloned.1.call-update) | async-done | bytes 4194320 | tf_op jit(solution)/shard_map/all_gather | solution.py:86
  104.2 6.4 %copy.16 = bf16[128,16384]{0,1:T(8,128)(2,1)} copy(bf16[128,16384]{1,0:T(8,128)(2,1)} %all-gather.10.cloned.1.call-done) | data formatting | bytes 8388608 | tf_op jit(solution)/shard_map/all_gather | solution.py:86
  110.6 57.6 %all_to_all.40 = bf16[128,8,2048]{0,2,1:T(8,128)(2,1)} all-to-all(bf16[128,8,2048]{0,2,1:T(8,128)(2,1)} %bitcast.91), channel_id=1, replica_groups=mesh['grp'=8,'vocab'=32] {'grp'}, dimensions={1} | all-to-all | bytes 8388608 | tf_op jit(solution)/shard_map/all_to_all | solution.py:89
  168.2 6.5 %copy.17 = bf16[8,128,2048]{2,1,0:T(8,128)(2,1)} copy(bf16[8,128,2048]{1,2,0:T(8,128)(2,1)} %bitcast.92) | data formatting | bytes 8388608 | tf_op jit(solution)/shard_map/all_to_all | solution.py:89
  174.6 14.4 %fusion.21 = f32[1024,2048]{1,0:T(8,128)} fusion(bf16[1024,2048]{1,0:T(8,128)(2,1)} %bitcast.93, bf16[2048,2048]{1,0:T(8,128)(2,1)} %param.10), kind=kOutput, calls=%fused_computation.58 | convolution fusion | flops 8589934592 | bytes 20971520 | tf_op jit(solution)/shard_map/dot_general | solution.py:94
  189.1 0.6 copy-done.1
  189.7 1.2 gather_fusion
  191.0 0.7 select_n.65
  191.6 4.2 all-to-all-start
  196.1 4.4 all-to-all-done
  201.0 0.7 reduce.6
  201.7 40.7 %reduce-scatter.2.cloned.1.call-done = f32[128,2048]{1,0:T(8,128)} async-done(((f32[1024,2048]{1,0:T(8,128)}), f32[128,2048]{1,0:T(8,128)}) %reduce-scatter.2.cloned.1.call-update) | async-done | bytes 1048592 | tf_op jit(solution)/shard_map/reduce_scatter | solution.py:93
  242.4 1.4 reduce_max.9
  243.8 31.7 %all-gather.4 = f32[32,1,128]{2,1,0:T(1,128)S(1)} all-gather(f32[1,1,128]{2,1,0:T(1,128)S(1)} %bitcast.100), channel_id=2, replica_groups=mesh['grp'=8,'vocab'=32] {'vocab'}, dimensions={0}, use_global_device_ids=true | all-gather | bytes 16896 | tf_op jit(solution)/shard_map/all_gather | solution.py:8
  275.4 1.7 fusion.11
  277.2 27.1 %all-gather.5 = f32[32,1,128]{2,1,0:T(1,128)S(1)} all-gather(f32[1,1,128]{2,1,0:T(1,128)S(1)} %bitcast.103), channel_id=3, replica_groups=mesh['grp'=8,'vocab'=32] {'vocab'}, dimensions={0}, use_global_device_ids=true | all-gather | bytes 16896 | tf_op jit(solution)/shard_map/all_gather | solution.py:8
  304.3 28.7 %all-gather.6 = f32[32,1,128]{2,1,0:T(1,128)S(1)} all-gather(f32[1,1,128]{2,1,0:T(1,128)S(1)} %bitcast.102), channel_id=4, replica_groups=mesh['grp'=8,'vocab'=32] {'vocab'}, dimensions={0}, use_global_device_ids=true | all-gather | bytes 16896 | tf_op jit(solution)/shard_map/all_gather | solution.py:8
  333.0 27.2 %all-gather.7 = f32[32,1,128]{2,1,0:T(1,128)S(1)} all-gather(f32[1,1,128]{2,1,0:T(1,128)S(1)} %bitcast.101), channel_id=5, replica_groups=mesh['grp'=8,'vocab'=32] {'vocab'}, dimensions={0}, use_global_device_ids=true | all-gather | bytes 16896 | tf_op jit(solution)/shard_map/all_gather | solution.py:8
  360.2 2.7 while.21
  362.9 56.7 %psum.7 = f32[128]{0:T(128)S(1)} all-reduce(f32[128]{0:T(128)S(1)} %get-tuple-element.232), channel_id=1, replica_groups=mesh['grp'=8,'vocab'=32] {'vocab'}, use_global_device_ids=true, to_apply=%region_5.6 | all-reduce | flops 128 | bytes 1024 | tf_op jit(solution)/shard_map/psum | solution.py:106
  419.6 0.7 all_to_all.33
  420.3 54.2 %all-to-all-start.3 = ((f32[8,1,16]{2,1,0:T(1,128)}), f32[8,1,16]{2,1,0:T(1,128)S(1)}, u32[]{:S(2)}, u32[]{:S(2)}) async-start(f32[8,1,16]{2,1,0:T(1,128)} %bitcast.28), calls=%async_computation.4 | async-start | bytes 8192 | tf_op jit(solution)/shard_map/all_to_all | solution.py:108
  474.5 4.6 all-to-all-done.3
  479.6 0.7 reduce.7
  480.3 1.0 scatter_custom_fusion.1
  481.5 0.5 fusion.18
  (129 shorter events, 3.9 us)
Async XLA Ops:
  7.2 3.6 copy-start
  7.2 97.0 %all-gather.10.cloned.1.call-start = ((), (), s32[]{:S(2)}) async-start(), calls=%async_computation.5 | async-start | bytes 4325376 | tf_op jit(solution)/shard_map/all_gather | solution.py:86
  23.3 219.1 %reduce-scatter.2.cloned.1.call-start = ((), (), s32[]{:S(2)}) async-start(), calls=%async_computation.6 | async-start | bytes 9437184 | tf_op jit(solution)/shard_map/reduce_scatter | solution.py:93
  189.1 0.7 copy-start.1
  189.1 6.8 %copy-start.4 = (s32[1,8]{1,0:T(1,128)S(1)}, s32[1,8]{1,0:T(1,128)}, u32[]{:S(2)}) copy-start(s32[1,8]{1,0:T(1,128)} %param.11) | copy-start | bytes 100
  189.1 285.4 %copy-start.2 = (s32[128,1]{0,1:T(1,128)S(1)}, s32[128,1]{0,1:T(1,128)}, u32[]{:S(2)}) copy-start(s32[128,1]{0,1:T(1,128)} %param.8) | copy-start | bytes 1540
  191.6 8.8 %all-to-all-start = ((s32[8,1,16]{2,1,0:T(1,128)}), s32[8,1,16]{2,1,0:T(1,128)S(1)}, u32[]{:S(2)}, u32[]{:S(2)}) async-start(s32[8,1,16]{2,1,0:T(1,128)} %bitcast.7), calls=%async_computation | async-start | bytes 8192 | tf_op jit(solution)/shard_map/all_to_all | solution.py:90
  419.6 62.5 %copy-start.3 = (f32[128]{0:T(128)}, f32[128]{0:T(128)S(1)}, u32[]{:S(2)}) copy-start(f32[128]{0:T(128)S(1)} %compare_select_fusion.2) | copy-start | bytes 1540
  420.3 58.8 %all-to-all-start.3 = ((f32[8,1,16]{2,1,0:T(1,128)}), f32[8,1,16]{2,1,0:T(1,128)S(1)}, u32[]{:S(2)}, u32[]{:S(2)}) async-start(f32[8,1,16]{2,1,0:T(1,128)} %bitcast.28), calls=%async_computation.4 | async-start | bytes 8192 | tf_op jit(solution)/shard_map/all_to_all | solution.py:108
Sparse Core Ops, SparseCore 0:
  23.4 80.6 all-gather.9
  189.2 53.1 reduce-scatter.1
where the time goes:
time: 490 us; the launch traced here: 489 us
  blocking collectives  241 us (49%)
  waiting for transfers between devices  130 us (27%)
  starting transfers between devices  58.5 us (12%)
  local copies, waits for them, and re-layouts  20.2 us (4%)
  matrix products  14.4 us (3%)
  between operations  14.2 us (3%)
  other arithmetic  9.6 us (2%)
    all_gather x4, blocking collectives, combined_all(): gathered = jax.tree.map(lambda a: lax.all_gather(a, axis), part)  115 us
    all_gather x1, waiting for transfers between devices, shards(): lax.all_gather(arrived.reshape(shard_rows, pieces.shape[1]), 'vocab', axi...  80.8 us
    all_to_all x1, blocking collectives, shards(): lax.all_to_all(full_rows, 'grp', split_axis=1, concat_axis=0, tiled=True)  57.6 us
    psum x1, blocking collectives, shards(): target_val = lax.psum(target_val, 'vocab')  56.7 us
    all_to_all x1, starting transfers between devices, shards(): lax.all_to_all(token_scores.reshape(groups, capacity), 'grp', split_axis=...  54.2 us
    reduce_scatter x1, waiting for transfers between devices, shards(): lax.psum_scatter(jnp.dot(block_rows, head, preferred_element_type=jnp.flo...  40.7 us
    dot_general x1, matrix products, shards(): jnp.dot(block_rows, head, preferred_element_type=jnp.float32)  14.4 us
    all_to_all x1, blocking collectives, shards(): lax.all_to_all(pieces.reshape(groups, capacity, pieces.shape[1]), 'grp',...  11.6 us
  transfers between devices with their start and end apart: 4, of which 4 were waited for; matrix products, arithmetic and copies ran while one was open for 1% of the time, Pallas kernels for 0%

commit v1 on v0

v1 whole, which is shorter than its diff:
```python
import jax
import jax.numpy as jnp
from jax import lax
from jax.experimental import pallas as pl
from jax.experimental.pallas import tpu as pltpu
from jax.sharding import PartitionSpec as P

MESH = pl.DeviceIdType.MESH
F32, BF16, I32, I16 = jnp.float32, jnp.bfloat16, jnp.int32, jnp.int16

NX, NC, NY, NZ = 4, 2, 4, 8
R = 128
FEAT = 512
HALF = FEAT // 2
KB = 2048
VB = 2048
TN = 512
NT = VB // TN
CAP = 16
OFF = (2, 1, 3, 0)
CODE_MAX = 32767.0
UNIT = 0.4375
EXT = 128

EARLY = tuple((k, s - k) for s in range(5) for k in range(4) if 0 <= s - k <= 4)
LATE = tuple((k, s - k) for s in range(5, 8) for k in range(4) if 0 <= s - k <= 4)


def rem(a, n):
    return lax.rem(a, jnp.int32(n))


def div(a, n):
    return lax.div(a, jnp.int32(n))


def body(
    hidden, head, flags, targets, lengths, tok_out, doc_out,
    X, W, Pb, PR, Q0, Q1, Q2, C0, C1, C2, stats, ST, SR, FS, FB, SS, SC, slots,
    w_sem, s1_send, s1_recv, z_send, z_recv, y_send, y_recv, p_send, p_recv,
    q_send, q_recv, st_send, st_recv, sc_send, sc_recv, f_send, f_recv,
):
    g = lax.axis_index("grp")
    v = lax.axis_index("vocab")
    x, c = div(g, NC), rem(g, NC)
    y, z = div(v, NZ), rem(v, NZ)
    rel = rem(z - 4 * c + NZ, NZ)
    h = rem(y, 2)
    plane = div(z, 4)

    def remote(src, dst, ss, rs, gg, vv):
        return pltpu.make_async_remote_copy(
            src_ref=src, dst_ref=dst, send_sem=ss, recv_sem=rs,
            device_id=(gg, vv), device_id_type=MESH,
        )

    def w_copy(j):
        return pltpu.make_async_copy(
            head.at[pl.ds(j * 512, 512)], W.at[pl.ds(j * 512, 512)], w_sem.at[j]
        )

    for j in range(4):
        w_copy(j).start()
    FS[...] = jnp.broadcast_to(flags[...], (8, R))

    barrier = pltpu.get_barrier_semaphore()

    def hello(gg, vv):
        pl.semaphore_signal(barrier, inc=1, device_id=(gg, vv), device_id_type=MESH)

    def hello_plane(i, _):
        hello(g, rem(v + i, NY * NZ))
        return 0

    def hello_grp(i, _):
        hello(rem(g + i, NX * NC), v)
        return 0

    lax.fori_loop(1, NX * NC, hello_grp, 0)

    @pl.when(plane == c)
    def _():
        def hello_source(r, _):
            @pl.when(jnp.logical_not((r == g) & (x == y)))
            def _():
                hello(r, x * NZ + z)
            return 0

        lax.fori_loop(0, NX * NC, hello_source, 0)

    lax.fori_loop(1, NY * NZ, hello_plane, 0)
    mine = ((x == y) & (plane == c)).astype(I32)
    pl.semaphore_wait(barrier, NY * NZ - 1 + NX * NC - 1 + NY - mine)

    g1 = y * 2 + plane
    j1 = rem(z, 4)

    def s1_refs(yy):
        hh = yy % 2
        return (
            hidden.at[:, pl.ds(hh * HALF, HALF)],
            X.at[g, :, pl.ds(pl.multiple_of(j1 * FEAT + hh * HALF, HALF), HALF)],
        )

    def s1_copy(yy):
        src, dst = s1_refs(yy)
        return remote(src, dst, s1_send.at[yy], s1_recv.at[g], g1, yy * NZ + z)

    def s1_self(yy):
        return (g1 == g) & (y == yy)

    for yy in range(NY):
        @pl.when(jnp.logical_not(s1_self(yy)))
        def _(yy=yy):
            s1_copy(yy).start()

        @pl.when(s1_self(yy))
        def _(yy=yy):
            src, dst = s1_refs(yy)
            pltpu.make_async_copy(src, dst, s1_recv.at[g]).start()

    def f_copy(i):
        return remote(FS, FB.at[g], f_send.at[i], f_recv.at[g], rem(g + i, NX * NC), v)

    def f_start(i, _):
        f_copy(i).start()
        return 0

    lax.fori_loop(1, NX * NC, f_start, 0)
    FB[g] = FS[...]

    def chunk_at(k):
        return rem(x + OFF[k], NX)

    def unit(k, cp, j, hh):
        col = pl.multiple_of(j * FEAT + hh * HALF, HALF)
        return X.at[2 * chunk_at(k) + cp, :, pl.ds(col, HALF)]

    def z_copy(k, t, way, cp, j):
        ref = unit(k, cp, j, h)
        to = rem(z + (1 if way == 0 else NZ - 1), NZ)
        return remote(ref, ref, z_send.at[k, t, way, cp], z_recv.at[k, cp, j], g, y * NZ + to)

    def y_copy(k, cp, j):
        ref = unit(k, cp, j, h)
        to = rem(y + (1 if cp == 0 else NY - 1), NY)
        return remote(ref, ref, y_send.at[k, cp, j], y_recv.at[k, cp, j], g, to * NZ + z)

    reach = ((4, 3), (3, 4))

    def origin(t, way):
        return rem(rel + (NZ - t if way == 0 else t), NZ)

    def event(k, t):
        if t == 0:
            @pl.when(rel < 4)
            def _():
                for cp in range(2):
                    r = 2 * chunk_at(k) + cp
                    ref = unit(k, cp, rel, h)
                    pltpu.make_async_copy(ref, ref, s1_recv.at[r]).wait()
                    z_copy(k, 0, 0, cp, rel).start()
                    z_copy(k, 0, 1, cp, rel).start()
                    y_copy(k, cp, rel).start()
            return
        for way in range(2):
            j = origin(t, way)

            @pl.when(j < 4)
            def _(way=way, j=j):
                for cp in range(2):
                    if t > reach[way][cp]:
                        continue
                    ref = unit(k, cp, j, h)
                    remote(ref, ref, z_send.at[k, 0, way, cp], z_recv.at[k, cp, j], g, v).wait_recv()
                    if t < reach[way][cp]:
                        z_copy(k, t, way, cp, j).start()
                    y_copy(k, cp, j).start()

    for k, t in EARLY:
        event(k, t)
    for j in range(4):
        w_copy(j).wait()

    def p_copy(k, n):
        cols = pl.ds(pl.multiple_of(n * TN, TN), TN)
        return remote(
            Pb.at[k, 1 - c, :, cols], PR.at[k, :, cols],
            p_send.at[k, n], p_recv.at[k, n], x * NC + (1 - c), v,
        )

    def wait_y(k):
        for cp in range(2):
            for j in range(4):
                ref = unit(k, cp, j, 1 - h)
                remote(ref, ref, y_send.at[k, cp, j], y_recv.at[k, cp, j], g, v).wait_recv()

    right, left = rem(x + 1, NX) * NC + c, rem(x + NX - 1, NX) * NC + c
    HV = VB // 2

    def q_copies(k):
        if k == 0:
            return (
                remote(Q0.at[0], C0.at[0], q_send.at[0], q_recv.at[0], right, v),
                remote(Q0.at[1], C0.at[1], q_send.at[1], q_recv.at[1], left, v),
            )
        if k == 1:
            return (remote(Q1, C1, q_send.at[2], q_recv.at[2], right, v),)
        return (remote(Q2, C2, q_send.at[3], q_recv.at[3], left, v),)

    def decode(block):
        wide = block.astype(I32).astype(F32)
        cols = wide.shape[1] - EXT
        step = wide[:, cols:cols + 1] * (UNIT / CODE_MAX)
        return wide[:, :cols] * step

    def encode(total):
        top = jnp.max(jnp.abs(total), axis=1, keepdims=True)
        scale = jnp.maximum(jnp.ceil(top * (1.0 / UNIT)), 1.0)
        codes = jnp.round(total * (CODE_MAX / (scale * UNIT)))
        return (
            codes.astype(I32).astype(I16),
            jnp.broadcast_to(scale, (total.shape[0], EXT)).astype(I32).astype(I16),
        )

    def pair_sum(k, rows):
        return Pb[k, c, rows, :] + PR[k, rows, :]

    def wait_pair(k):
        for n in range(NT):
            p_copy(k, n).wait_recv()

    def post(k):
        wait_pair(k)
        if k == 1:
            q_copies(0)[0].wait_recv()
        if k == 2:
            q_copies(0)[1].wait_recv()

        @pl.loop(0, R // 16)
        def _(i):
            rows = pl.ds(pl.multiple_of(i * 16, 16), 16)
            total = pair_sum(k, rows)
            if k == 0:
                codes, scale = encode(total)
                for side in range(2):
                    Q0[side, rows, :HV] = codes[:, side * HV:(side + 1) * HV]
                    Q0[side, rows, HV:] = scale
            else:
                first, second = total[:, :HV], total[:, HV:]
                if k == 1:
                    first = first + decode(C0[0, rows, :])
                else:
                    second = second + decode(C0[1, rows, :])
                codes, scale = encode(jnp.concatenate([first, second], axis=1))
                out = Q1 if k == 1 else Q2
                out[rows, :VB] = codes
                out[rows, VB:] = scale

        for copy in q_copies(k):
            copy.start()

    late = {}
    for at, ev in enumerate(LATE):
        late.setdefault(at, []).append(ev)

    def tile(step, _):
        k, n = div(step, NT), rem(step, NT)
        for kk in range(4):
            @pl.when(step == kk * NT)
            def _(kk=kk):
                wait_y(kk)
        d = rem(x + jnp.where(k == 0, 2, jnp.where(k == 1, 1, jnp.where(k == 2, 3, 0))), NX)
        cols = pl.ds(pl.multiple_of(n * TN, TN), TN)
        rows = X[pl.ds(2 * d, 2)].reshape(2 * R, KB)
        out = jnp.dot(rows, W[:, cols], preferred_element_type=F32)
        Pb[k, :, :, cols] = out.reshape(2, R, TN)
        p_copy(k, n).start()
        for at, events in late.items():
            @pl.when(step == at)
            def _(events=events):
                for ev in events:
                    event(*ev)
        for kk in range(3):
            @pl.when(step == (kk + 1) * NT + 1)
            def _(kk=kk):
                post(kk)
        return 0

    lax.fori_loop(0, 4 * NT, tile, 0)

    def f_wait(i, _):
        gg = rem(g + i, NX * NC)
        remote(FS, FB.at[gg], f_send.at[0], f_recv.at[gg], gg, v).wait_recv()
        return 0

    lax.fori_loop(1, NX * NC, f_wait, 0)
    named = FB[:, 0, :] == g
    above = (
        lax.broadcasted_iota(I32, (R, R), 0) < lax.broadcasted_iota(I32, (R, R), 1)
    ).astype(BF16)
    rank = jnp.dot(named.astype(F32).astype(BF16), above, preferred_element_type=F32)
    shard = lax.broadcasted_iota(I32, (8, R), 0)
    slots[...] = jnp.where(named, shard * CAP + rank.astype(I32), -1)

    wait_pair(3)
    q_copies(1)[0].wait_recv()
    q_copies(2)[0].wait_recv()
    want = jnp.transpose(jnp.broadcast_to(targets[...].astype(F32), (R, R)))
    stats[...] = want

    @pl.loop(0, R // 16)
    def _(i):
        rows = pl.ds(pl.multiple_of(i * 16, 16), 16)
        logits = pair_sum(3, rows) + decode(C1[rows, :]) + decode(C2[rows, :])
        target = stats[rows, :][:, :1].astype(I32) - v * VB
        top = jnp.max(logits, axis=1, keepdims=True)
        shifted = logits - top
        scaled = jnp.exp(shifted)
        first = scaled * shifted
        total = jnp.sum(scaled, axis=1, keepdims=True)
        mom1 = jnp.sum(first, axis=1, keepdims=True)
        mom2 = jnp.sum(first * shifted, axis=1, keepdims=True)
        column = lax.broadcasted_iota(I32, (16, VB), 1)
        val = jnp.sum(jnp.where(column == target, logits, 0.0), axis=1, keepdims=True)
        lane = lax.broadcasted_iota(I32, (16, R), 1)
        stats[rows, :] = jnp.where(
            lane == 0, top,
            jnp.where(lane == 1, total, jnp.where(lane == 2, mom1, jnp.where(lane == 3, mom2, val))),
        )

    ST[...] = jnp.transpose(stats[...])[:8, :]
    SR[v] = ST[...]

    def st_copy(i):
        return remote(ST, SR.at[v], st_send.at[i], st_recv.at[v], g, rem(v + i, NY * NZ))

    def st_start(i, _):
        st_copy(i).start()
        return 0

    lax.fori_loop(1, NY * NZ, st_start, 0)

    def st_wait(i, _):
        vv = rem(v + i, NY * NZ)
        remote(ST, SR.at[vv], st_send.at[0], st_recv.at[vv], g, v).wait_recv()
        return 0

    lax.fori_loop(1, NY * NZ, st_wait, 0)
    tops = SR[:, 0, :]
    top = jnp.max(tops, axis=0, keepdims=True)
    gap = tops - top
    fac = jnp.exp(gap)
    tot, m1, m2 = SR[:, 1, :], SR[:, 2, :], SR[:, 3, :]
    total = jnp.sum(fac * tot, axis=0, keepdims=True)
    mom1 = jnp.sum(fac * (m1 + gap * tot), axis=0, keepdims=True)
    mom2 = jnp.sum(fac * (m2 + 2.0 * gap * m1 + gap * gap * tot), axis=0, keepdims=True)
    val = jnp.sum(SR[:, 4, :], axis=0, keepdims=True)
    mean = mom1 / total
    var = mom2 / total - mean * mean
    score = (val - top - mean) / jnp.sqrt(jnp.maximum(var, 1.0))

    SS[...] = jnp.broadcast_to(score, (8, R))
    SC[g] = SS[...]

    def sc_copy(i):
        return remote(SS, SC.at[g], sc_send.at[i], sc_recv.at[g], rem(g + i, NX * NC), v)

    def sc_start(i, _):
        sc_copy(i).start()
        return 0

    lax.fori_loop(1, NX * NC, sc_start, 0)

    ends_of = jnp.broadcast_to(lengths[...], (8, 8))
    doc = lax.broadcasted_iota(I32, (8, 8), 0)
    at = lax.broadcasted_iota(I32, (8, 8), 1)
    ends = jnp.sum(jnp.where(at <= doc, ends_of, 0), axis=1, keepdims=True)
    starts = jnp.sum(jnp.where(at < doc, ends_of, 0), axis=1, keepdims=True)
    position = lax.broadcasted_iota(I32, (8, R), 1)
    member = (position >= starts) & (position < ends) & (flags[...] < NX * NC)
    sums = jnp.sum(jnp.where(member, SS[...], 0.0), axis=1, keepdims=True)
    counts = jnp.sum(jnp.where(member, 1.0, 0.0), axis=1, keepdims=True)
    means = sums / jnp.maximum(counts, 1.0)
    doc_out[...] = jnp.sum(jnp.where(at == doc, means, 0.0), axis=0, keepdims=True)

    def sc_wait(i, _):
        gg = rem(g + i, NX * NC)
        remote(SS, SC.at[gg], sc_send.at[0], sc_recv.at[gg], gg, v).wait_recv()
        return 0

    lax.fori_loop(1, NX * NC, sc_wait, 0)
    place = lax.broadcasted_iota(I32, (R, R), 0)
    spread = jnp.zeros((R, R), F32)
    for s in range(8):
        spread = spread + jnp.where(slots[s:s + 1, :] == place, SC[s, 0:1, :], 0.0)
    tok_out[...] = jnp.sum(jnp.transpose(spread), axis=0, keepdims=True)

    for yy in range(NY):
        @pl.when(jnp.logical_not(s1_self(yy)))
        def _(yy=yy):
            s1_copy(yy).wait_send()

    for k in range(4):
        @pl.when(rel < 4)
        def _(k=k):
            for cp in range(2):
                z_copy(k, 0, 0, cp, rel).wait_send()
                z_copy(k, 0, 1, cp, rel).wait_send()
        for t in range(1, 4):
            for way in range(2):
                j = origin(t, way)

                @pl.when(j < 4)
                def _(k=k, t=t, way=way, j=j):
                    for cp in range(2):
                        if t < reach[way][cp]:
                            z_copy(k, t, way, cp, j).wait_send()
        for cp in range(2):
            for j in range(4):
                y_copy(k, cp, j).wait_send()
        for n in range(NT):
            p_copy(k, n).wait_send()
        if k < 3:
            for copy in q_copies(k):
                copy.wait_send()

    def st_sent(i, _):
        st_copy(i).wait_send()
        return 0

    def sc_sent(i, _):
        f_copy(i).wait_send()
        sc_copy(i).wait_send()
        return 0

    lax.fori_loop(1, NY * NZ, st_sent, 0)
    lax.fori_loop(1, NX * NC, sc_sent, 0)


def shards(hidden, flags, targets, head, lengths):
    vmem = pl.BlockSpec(memory_space=pltpu.VMEM)
    anywhere = pl.BlockSpec(memory_space=pl.ANY)
    dma = pltpu.SemaphoreType.DMA
    tok, doc = pl.pallas_call(
        body,
        out_shape=(
            jax.ShapeDtypeStruct((1, R), F32),
            jax.ShapeDtypeStruct((1, 8), F32),
        ),
        in_specs=[anywhere, anywhere, vmem, vmem, vmem],
        out_specs=(vmem, vmem),
        scratch_shapes=[
            pltpu.VMEM((8, R, KB), BF16),
            pltpu.VMEM((KB, VB), BF16),
            pltpu.VMEM((4, 2, R, VB), F32),
            pltpu.VMEM((4, R, VB), F32),
            pltpu.VMEM((2, R, VB // 2 + EXT), I16),
            pltpu.VMEM((R, VB + EXT), I16),
            pltpu.VMEM((R, VB + EXT), I16),
            pltpu.VMEM((2, R, VB // 2 + EXT), I16),
            pltpu.VMEM((R, VB + EXT), I16),
            pltpu.VMEM((R, VB + EXT), I16),
            pltpu.VMEM((R, R), F32),
            pltpu.VMEM((8, R), F32),
            pltpu.VMEM((NY * NZ, 8, R), F32),
            pltpu.VMEM((8, R), I32),
            pltpu.VMEM((8, 8, R), I32),
            pltpu.VMEM((8, R), F32),
            pltpu.VMEM((8, 8, R), F32),
            pltpu.VMEM((8, R), I32),
            dma((4,)), dma((4,)), dma((8,)),
            dma((4, 4, 2, 2)), dma((4, 2, 4)),
            dma((4, 2, 4)), dma((4, 2, 4)),
            dma((4, NT)), dma((4, NT)),
            dma((4,)), dma((4,)),
            dma((32,)), dma((32,)),
            dma((8,)), dma((8,)), dma((8,)), dma((8,)),
        ],
        compiler_params=pltpu.CompilerParams(
            collective_id=0, has_side_effects=True, vmem_limit_bytes=60 * 1024 * 1024
        ),
        name="score",
    )(hidden, head, flags.reshape(1, R), targets.reshape(1, R), lengths)
    return tok.reshape(R), doc


def solution(mesh):
    placed = (P("grp", "vocab"), P("grp", None), P("grp"), P("grp", "vocab"), P("grp", None))
    return jax.shard_map(
        shards, mesh=mesh, in_specs=placed, out_specs=(P("grp"), P("grp", None)), check_vma=False
    )
```

time: 490 us -> 101 us (0.21)
  blocking collectives: 241 us -> 0 us
  waiting for transfers between devices: 130 us -> 0 us
  Pallas kernels: 0 us -> 98.3 us
  starting transfers between devices: 58.5 us -> 0 us
  local copies, waits for them, and re-layouts: 20.2 us -> 2.25 us
  matrix products: 14.4 us -> 0 us
  between operations: 14.2 us -> 0.64 us
  other arithmetic: 9.6 us -> 0 us
    all_gather x4 -> x0, blocking collectives: 115 us -> none  [combined_all(): gathered = jax.tree.map(lambda a: lax.all_gather(a, axis), part)]
    pallas_call x0 -> x1, Pallas kernels: none -> 98.3 us  [shards(): pl.pallas_call(body, out_shape=(jax.ShapeDtypeStruct((1, R), F32), jax.Sh...]
    all_gather x1 -> x0, waiting for transfers between devices: 80.8 us -> none  [shards(): lax.all_gather(arrived.reshape(shard_rows, pieces.shape[1]), 'vocab', axi...]
    all_to_all x2 -> x0, blocking collectives: 69.2 us -> none  [the longest x1 57.6 us: shards(): lax.all_to_all(full_rows, 'grp', split_axis=1, concat_axis=0, tiled=True)]
    all_to_all x2 -> x0, starting transfers between devices: 58.5 us -> none  [the longest x1 54.2 us: shards(): lax.all_to_all(token_scores.reshape(groups, capacity), 'grp', split_axis=...]
    psum x1 -> x0, blocking collectives: 56.7 us -> none  [shards(): target_val = lax.psum(target_val, 'vocab')]
    reduce_scatter x1 -> x0, waiting for transfers between devices: 40.7 us -> none  [shards(): lax.psum_scatter(jnp.dot(block_rows, head, preferred_element_type=jnp.flo...]
    dot_general x1 -> x0, matrix products: 14.4 us -> none  [shards(): jnp.dot(block_rows, head, preferred_element_type=jnp.float32)]
  transfers between devices with their start and end apart: 4 -> 0, of which waited for: 4 -> 0; matrix products, arithmetic and copies ran while one was open for 1% -> 0% of each run, Pallas kernels for 0% -> 0%
where the time goes in v1:
time: 101 us
  Pallas kernels  98.3 us (97%)
  local copies, waits for them, and re-layouts  2.25 us (2%)
    pallas_call x1, Pallas kernels, shards(): pl.pallas_call(body, out_shape=(jax.ShapeDtypeStruct((1, R), F32), jax.Sh...  98.3 us
    unnamed x2, local copies, waits for them, and re-layouts  2.25 us

profile of v1, /device:TPU:1, one launch (start us, length us, event | category | flops | bytes accessed | tf_op | source)
XLA Modules:
  0.0 101.2 jit_solution(16816554660547938285)
XLA Ops:
  0.6 98.3 %score.1 = (f32[1,128]{1,0:T(1,128)}, f32[1,8]{1,0:T(1,128)}) custom-call(bf16[128,512]{1,0:T(8,128)(2,1)} %hidden.1, bf16[2048,2048]{1,0:T(8,128)(2,1)} %head.1, s32[1,128]{1,0:T(1,128)} %bitcast.3, s32[1,128]{1,0:T(1,128)} %bitcast.4, s32[1,8]{1,0:T(1,128)} %lengths.1), custom_call_target="tpu_custom_call" | custom-call | tf_op jit(solution)/shard_map/score/pallas_call | solution.py:445
  99.0 1.1 %copy.9 = f32[128]{0:T(128)} copy(f32[128]{0:T(128)} %bitcast.5) | data formatting | bytes 1024
  100.1 1.1 %copy.10 = f32[1,8]{1,0:T(1,128)} copy(f32[1,8]{1,0:T(1,128)} %get-tuple-element.9) | data formatting | bytes 64

commit v2 on v1

--- a/solution.py
+++ b/solution.py
@@ -22,8 +22,12 @@
 UNIT = 0.4375
 EXT = 128
 
-EARLY = tuple((k, s - k) for s in range(5) for k in range(4) if 0 <= s - k <= 4)
-LATE = tuple((k, s - k) for s in range(5, 8) for k in range(4) if 0 <= s - k <= 4)
+HV = VB // 2
+
+ORDER = sorted(((k, t) for k in range(4) for t in range(5)), key=lambda e: (2 * e[1] + e[0], e[0]))
+EARLY = tuple(ORDER[:16])
+LATE = {0: (ORDER[16],), 1: (ORDER[17],), 3: (ORDER[18],), 6: (ORDER[19],)}
+POSTS = {3: ((0, 0),), 5: ((0, 1),), 7: ((1, 1),), 11: ((2, 0), (1, 0)), 13: ((2, 1),)}
 
 
 def rem(a, n):
@@ -35,9 +39,9 @@
 
 
 def body(
-    hidden, head, flags, targets, lengths, tok_out, doc_out,
-    X, W, Pb, PR, Q0, Q1, Q2, C0, C1, C2, stats, ST, SR, FS, FB, SS, SC, slots,
-    w_sem, s1_send, s1_recv, z_send, z_recv, y_send, y_recv, p_send, p_recv,
+    hidden, head, flags, targets, lengths, result,
+    X, W, H, Pb, PR, Q, C, stats, ST, SR, FS, FB, SS, SC, slots,
+    w_sem, h_send, h_recv, s1_send, s1_recv, z_send, z_recv, y_send, y_recv, p_send, p_recv,
     q_send, q_recv, st_send, st_recv, sc_send, sc_recv, f_send, f_recv,
 ):
     g = lax.axis_index("grp")
@@ -59,6 +63,10 @@
             head.at[pl.ds(j * 512, 512)], W.at[pl.ds(j * 512, 512)], w_sem.at[j]
         )
 
+    def half_of(side):
+        return hidden.at[:, pl.ds(pl.multiple_of(side * HALF, HALF), HALF)]
+
+    pltpu.make_async_copy(half_of(h), H.at[y], h_recv.at[y]).start()
     for j in range(4):
         w_copy(j).start()
     FS[...] = jnp.broadcast_to(flags[...], (8, R))
@@ -78,46 +86,43 @@
 
     lax.fori_loop(1, NX * NC, hello_grp, 0)
 
-    @pl.when(plane == c)
-    def _():
-        def hello_source(r, _):
-            @pl.when(jnp.logical_not((r == g) & (x == y)))
-            def _():
-                hello(r, x * NZ + z)
-            return 0
-
-        lax.fori_loop(0, NX * NC, hello_source, 0)
-
     lax.fori_loop(1, NY * NZ, hello_plane, 0)
-    mine = ((x == y) & (plane == c)).astype(I32)
-    pl.semaphore_wait(barrier, NY * NZ - 1 + NX * NC - 1 + NY - mine)
-
-    g1 = y * 2 + plane
+    pl.semaphore_wait(barrier, NY * NZ - 1 + NX * NC - 1)
+
     j1 = rem(z, 4)
 
-    def s1_refs(yy):
-        hh = yy % 2
-        return (
-            hidden.at[:, pl.ds(hh * HALF, HALF)],
-            X.at[g, :, pl.ds(pl.multiple_of(j1 * FEAT + hh * HALF, HALF), HALF)],
-        )
-
-    def s1_copy(yy):
-        src, dst = s1_refs(yy)
-        return remote(src, dst, s1_send.at[yy], s1_recv.at[g], g1, yy * NZ + z)
-
-    def s1_self(yy):
-        return (g1 == g) & (y == yy)
-
-    for yy in range(NY):
-        @pl.when(jnp.logical_not(s1_self(yy)))
-        def _(yy=yy):
-            s1_copy(yy).start()
-
-        @pl.when(s1_self(yy))
-        def _(yy=yy):
-            src, dst = s1_refs(yy)
+    def h_copy(i):
+        yy = rem(y + i, NY)
+        return remote(half_of(rem(yy, 2)), H.at[y], h_send.at[i], h_recv.at[y], g, yy * NZ + z)
+
+    for i in (2, 1, 3):
+        h_copy(i).start()
+
+    def s1_owner(i):
+        return rem(x + i, NX) * NC + plane
+
+    def s1_refs(i):
+        col = pl.multiple_of(j1 * FEAT + h * HALF, HALF)
+        return H.at[rem(x + i, NX)], X.at[g, :, pl.ds(col, HALF)]
+
+    def s1_copy(i):
+        src, dst = s1_refs(i)
+        return remote(src, dst, s1_send.at[i], s1_recv.at[g], s1_owner(i), v)
+
+    for i in (2, 3, 1, 0):
+        src, dst = s1_refs(i)
+        pltpu.make_async_copy(src, src, h_recv.at[rem(x + i, NX)]).wait()
+        if i:
+            s1_copy(i).start()
+            continue
+
+        @pl.when(plane == c)
+        def _(src=src, dst=dst):
             pltpu.make_async_copy(src, dst, s1_recv.at[g]).start()
+
+        @pl.when(plane != c)
+        def _():
+            s1_copy(0).start()
 
     def f_copy(i):
         return remote(FS, FB.at[g], f_send.at[i], f_recv.at[g], rem(g + i, NX * NC), v)
@@ -196,23 +201,15 @@
                 remote(ref, ref, y_send.at[k, cp, j], y_recv.at[k, cp, j], g, v).wait_recv()
 
     right, left = rem(x + 1, NX) * NC + c, rem(x + NX - 1, NX) * NC + c
-    HV = VB // 2
-
-    def q_copies(k):
-        if k == 0:
-            return (
-                remote(Q0.at[0], C0.at[0], q_send.at[0], q_recv.at[0], right, v),
-                remote(Q0.at[1], C0.at[1], q_send.at[1], q_recv.at[1], left, v),
-            )
-        if k == 1:
-            return (remote(Q1, C1, q_send.at[2], q_recv.at[2], right, v),)
-        return (remote(Q2, C2, q_send.at[3], q_recv.at[3], left, v),)
-
-    def decode(block):
-        wide = block.astype(I32).astype(F32)
-        cols = wide.shape[1] - EXT
-        step = wide[:, cols:cols + 1] * (UNIT / CODE_MAX)
-        return wide[:, :cols] * step
+
+    def q_copy(k, hf):
+        u = 2 * k + hf
+        to = right if k == 1 or (k == 0 and hf == 0) else left
+        return remote(Q.at[u], C.at[u], q_send.at[u], q_recv.at[u], to, v)
+
+    def decode(u, rows):
+        wide = C[u, rows, :].astype(I32).astype(F32)
+        return wide[:, :HV] * (wide[:, HV:HV + 1] * (UNIT / CODE_MAX))
 
     def encode(total):
         top = jnp.max(jnp.abs(total), axis=1, keepdims=True)
@@ -223,49 +220,36 @@
             jnp.broadcast_to(scale, (total.shape[0], EXT)).astype(I32).astype(I16),
         )
 
-    def pair_sum(k, rows):
-        return Pb[k, c, rows, :] + PR[k, rows, :]
-
-    def wait_pair(k):
-        for n in range(NT):
+    def pair_sum(k, rows, hf):
+        cols = slice(hf * HV, (hf + 1) * HV)
+        return Pb[k, c, rows, cols] + PR[k, rows, cols]
+
+    def wait_pair(k, hf):
+        for n in (2 * hf, 2 * hf + 1):
             p_copy(k, n).wait_recv()
 
-    def post(k):
-        wait_pair(k)
-        if k == 1:
-            q_copies(0)[0].wait_recv()
-        if k == 2:
-            q_copies(0)[1].wait_recv()
+    def post(k, hf):
+        wait_pair(k, hf)
+        relayed = k == hf + 1
+        if relayed:
+            q_copy(0, hf).wait_recv()
+        u = 2 * k + hf
 
         @pl.loop(0, R // 16)
         def _(i):
             rows = pl.ds(pl.multiple_of(i * 16, 16), 16)
-            total = pair_sum(k, rows)
-            if k == 0:
-                codes, scale = encode(total)
-                for side in range(2):
-                    Q0[side, rows, :HV] = codes[:, side * HV:(side + 1) * HV]
-                    Q0[side, rows, HV:] = scale
-            else:
-                first, second = total[:, :HV], total[:, HV:]
-                if k == 1:
-                    first = first + decode(C0[0, rows, :])
-                else:
-                    second = second + decode(C0[1, rows, :])
-                codes, scale = encode(jnp.concatenate([first, second], axis=1))
-                out = Q1 if k == 1 else Q2
-                out[rows, :VB] = codes
-                out[rows, VB:] = scale
-
-        for copy in q_copies(k):
-            copy.start()
-
-    late = {}
-    for at, ev in enumerate(LATE):
-        late.setdefault(at, []).append(ev)
+            total = pair_sum(k, rows, hf)
+            if relayed:
+                total = total + decode(hf, rows)
+            codes, scale = encode(total)
+            Q[u, rows, :HV] = codes
+            Q[u, rows, HV:] = scale
+
+        q_copy(k, hf).start()
 
     def tile(step, _):
-        k, n = div(step, NT), rem(step, NT)
+        k = div(step, NT)
+        n = rem(step + jnp.where(k == 1, 2, 0), NT)
         for kk in range(4):
             @pl.when(step == kk * NT)
             def _(kk=kk):
@@ -276,15 +260,16 @@
         out = jnp.dot(rows, W[:, cols], preferred_element_type=F32)
         Pb[k, :, :, cols] = out.reshape(2, R, TN)
         p_copy(k, n).start()
-        for at, events in late.items():
+        for at, events in LATE.items():
             @pl.when(step == at)
             def _(events=events):
                 for ev in events:
                     event(*ev)
-        for kk in range(3):
-            @pl.when(step == (kk + 1) * NT + 1)
-            def _(kk=kk):
-                post(kk)
+        for at, blocks in POSTS.items():
+            @pl.when(step == at)
+            def _(blocks=blocks):
+                for block in blocks:
+                    post(*block)
         return 0
 
     lax.fori_loop(0, 4 * NT, tile, 0)
@@ -303,16 +288,25 @@
     shard = lax.broadcasted_iota(I32, (8, R), 0)
     slots[...] = jnp.where(named, shard * CAP + rank.astype(I32), -1)
 
-    wait_pair(3)
-    q_copies(1)[0].wait_recv()
-    q_copies(2)[0].wait_recv()
+    for hf in range(2):
+        wait_pair(3, hf)
     want = jnp.transpose(jnp.broadcast_to(targets[...].astype(F32), (R, R)))
     stats[...] = want
+    for hf in (1, 0):
+        q_copy(1, hf).wait_recv()
+
+        @pl.loop(0, R // 16)
+        def _(i, hf=hf):
+            rows = pl.ds(pl.multiple_of(i * 16, 16), 16)
+            PR[3, rows, hf * HV:(hf + 1) * HV] = pair_sum(3, rows, hf) + decode(2 + hf, rows)
+
+    for hf in range(2):
+        q_copy(2, hf).wait_recv()
 
     @pl.loop(0, R // 16)
     def _(i):
         rows = pl.ds(pl.multiple_of(i * 16, 16), 16)
-        logits = pair_sum(3, rows) + decode(C1[rows, :]) + decode(C2[rows, :])
+        logits = PR[3, rows, :] + jnp.concatenate([decode(4, rows), decode(5, rows)], axis=1)
         target = stats[rows, :][:, :1].astype(I32) - v * VB
         top = jnp.max(logits, axis=1, keepdims=True)
         shifted = logits - top
@@ -382,7 +376,8 @@
     sums = jnp.sum(jnp.where(member, SS[...], 0.0), axis=1, keepdims=True)
     counts = jnp.sum(jnp.where(member, 1.0, 0.0), axis=1, keepdims=True)
     means = sums / jnp.maximum(counts, 1.0)
-    doc_out[...] = jnp.sum(jnp.where(at == doc, means, 0.0), axis=0, keepdims=True)
+    place = lax.broadcasted_iota(I32, (8, R), 0)
+    result[:, R:] = jnp.sum(jnp.where(position == place, means, 0.0), axis=0, keepdims=True)
 
     def sc_wait(i, _):
         gg = rem(g + i, NX * NC)
@@ -394,12 +389,15 @@
     spread = jnp.zeros((R, R), F32)
     for s in range(8):
         spread = spread + jnp.where(slots[s:s + 1, :] == place, SC[s, 0:1, :], 0.0)
-    tok_out[...] = jnp.sum(jnp.transpose(spread), axis=0, keepdims=True)
-
-    for yy in range(NY):
-        @pl.when(jnp.logical_not(s1_self(yy)))
-        def _(yy=yy):
-            s1_copy(yy).wait_send()
+    result[:, :R] = jnp.sum(jnp.transpose(spread), axis=0, keepdims=True)
+
+    for i in range(1, 4):
+        h_copy(i).wait_send()
+        s1_copy(i).wait_send()
+
+    @pl.when(plane != c)
+    def _():
+        s1_copy(0).wait_send()
 
     for k in range(4):
         @pl.when(rel < 4)
@@ -422,8 +420,8 @@
         for n in range(NT):
             p_copy(k, n).wait_send()
         if k < 3:
-            for copy in q_copies(k):
-                copy.wait_send()
+            for hf in range(2):
+                q_copy(k, hf).wait_send()
 
     def st_sent(i, _):
         st_copy(i).wait_send()
@@ -442,25 +440,19 @@
     vmem = pl.BlockSpec(memory_space=pltpu.VMEM)
     anywhere = pl.BlockSpec(memory_space=pl.ANY)
     dma = pltpu.SemaphoreType.DMA
-    tok, doc = pl.pallas_call(
+    out = pl.pallas_call(
         body,
-        out_shape=(
-            jax.ShapeDtypeStruct((1, R), F32),
-            jax.ShapeDtypeStruct((1, 8), F32),
-        ),
+        out_shape=jax.ShapeDtypeStruct((1, 2 * R), F32),
         in_specs=[anywhere, anywhere, vmem, vmem, vmem],
-        out_specs=(vmem, vmem),
+        out_specs=vmem,
         scratch_shapes=[
             pltpu.VMEM((8, R, KB), BF16),
             pltpu.VMEM((KB, VB), BF16),
+            pltpu.VMEM((NY, R, HALF), BF16),
             pltpu.VMEM((4, 2, R, VB), F32),
             pltpu.VMEM((4, R, VB), F32),
-            pltpu.VMEM((2, R, VB // 2 + EXT), I16),
-            pltpu.VMEM((R, VB + EXT), I16),
-            pltpu.VMEM((R, VB + EXT), I16),
-            pltpu.VMEM((2, R, VB // 2 + EXT), I16),
-            pltpu.VMEM((R, VB + EXT), I16),
-            pltpu.VMEM((R, VB + EXT), I16),
+            pltpu.VMEM((6, R, HV + EXT), I16),
+            pltpu.VMEM((6, R, HV + EXT), I16),
             pltpu.VMEM((R, R), F32),
             pltpu.VMEM((8, R), F32),
             pltpu.VMEM((NY * NZ, 8, R), F32),
@@ -469,11 +461,11 @@
             pltpu.VMEM((8, R), F32),
             pltpu.VMEM((8, 8, R), F32),
             pltpu.VMEM((8, R), I32),
-            dma((4,)), dma((4,)), dma((8,)),
+            dma((4,)), dma((4,)), dma((4,)), dma((4,)), dma((8,)),
             dma((4, 4, 2, 2)), dma((4, 2, 4)),
             dma((4, 2, 4)), dma((4, 2, 4)),
             dma((4, NT)), dma((4, NT)),
-            dma((4,)), dma((4,)),
+            dma((6,)), dma((6,)),
             dma((32,)), dma((32,)),
             dma((8,)), dma((8,)), dma((8,)), dma((8,)),
         ],
@@ -482,7 +474,7 @@
         ),
         name="score",
     )(hidden, head, flags.reshape(1, R), targets.reshape(1, R), lengths)
-    return tok.reshape(R), doc
+    return out[0, :R], out[:, R:R + 8]
 
 
 def solution(mesh):

time: 101 us -> 93.1 us (0.922)
  Pallas kernels: 98.3 us -> 90 us
    pallas_call x1, Pallas kernels: 98.3 us -> 90 us  [shards(): pl.pallas_call(body, out_shape=jax.ShapeDtypeStruct((1, 2 * R), F32), in_...]
    unnamed x2 -> x0, local copies, waits for them, and re-layouts: 2.25 us -> none
    squeeze x0 -> x1, local copies, waits for them, and re-layouts: none -> 1.19 us  [shards(): return (out[0, :R], out[:, R:R + 8])]
    slice x0 -> x1, local copies, waits for them, and re-layouts: none -> 1.09 us  [shards(): return (out[0, :R], out[:, R:R + 8])]
where the time goes in v2:
time: 93.1 us; the launch traced here: 93 us
  Pallas kernels  90 us (97%)
  local copies, waits for them, and re-layouts  2.28 us (2%)
    pallas_call x1, Pallas kernels, shards(): pl.pallas_call(body, out_shape=jax.ShapeDtypeStruct((1, 2 * R), F32), in_...  90 us

profile of v2, /device:TPU:1, one launch (start us, length us, event | category | flops | bytes accessed | tf_op | source)
XLA Modules:
  0.0 93.0 jit_solution(2324425639739933815)
XLA Ops:
  0.6 90.0 %score.1 = f32[1,256]{1,0:T(1,128)} custom-call(bf16[128,512]{1,0:T(8,128)(2,1)} %hidden.1, bf16[2048,2048]{1,0:T(8,128)(2,1)} %head.1, s32[1,128]{1,0:T(1,128)} %bitcast.4, s32[1,128]{1,0:T(1,128)} %bitcast.5, s32[1,8]{1,0:T(1,128)} %lengths.1), custom_call_target="tpu_custom_call" | custom-call | tf_op jit(solution)/shard_map/score/pallas_call | solution.py:443
  90.7 1.1 %slice.7 = f32[1,8]{1,0:T(1,128)} slice(f32[1,256]{1,0:T(1,128)} %score.1), slice={[0:1], [128:136]} | slice | bytes 64 | tf_op jit(solution)/shard_map/slice | solution.py:477
  91.8 1.2 %slice_bitcast_fusion = f32[128]{0:T(128)} fusion(f32[1,256]{1,0:T(1,128)} %score.1), kind=kLoop, calls=%fused_computation | loop fusion | bytes 1024 | tf_op jit(solution)/shard_map/squeeze | solution.py:477

commit v3 on v2

--- a/solution.py
+++ b/solution.py
@@ -24,7 +24,7 @@
 
 HV = VB // 2
 
-ORDER = sorted(((k, t) for k in range(4) for t in range(5)), key=lambda e: (2 * e[1] + e[0], e[0]))
+ORDER = sorted(((k, t) for k in range(4) for t in range(5)), key=lambda e: (3 * e[1] + 2 * e[0], e[0]))
 EARLY = tuple(ORDER[:16])
 LATE = {0: (ORDER[16],), 1: (ORDER[17],), 3: (ORDER[18],), 6: (ORDER[19],)}
 POSTS = {3: ((0, 0),), 5: ((0, 1),), 7: ((1, 1),), 11: ((2, 0), (1, 0)), 13: ((2, 1),)}

time: 93.1 us -> 91.7 us (0.985)
  Pallas kernels: 90 us -> 88.7 us
    pallas_call x1, Pallas kernels: 90 us -> 88.7 us  [shards(): pl.pallas_call(body, out_shape=jax.ShapeDtypeStruct((1, 2 * R), F32), in_...]
where the time goes in v3:
time: 91.7 us; the launch traced here: 91.6 us
  Pallas kernels  88.7 us (97%)
  local copies, waits for them, and re-layouts  2.28 us (2%)
    pallas_call x1, Pallas kernels, shards(): pl.pallas_call(body, out_shape=jax.ShapeDtypeStruct((1, 2 * R), F32), in_...  88.7 us

profile of v3, /device:TPU:1, one launch (start us, length us, event | category | flops | bytes accessed | tf_op | source)
XLA Modules:
  0.0 91.6 jit_solution(1757742999424549435)
XLA Ops:
  0.6 88.7 %score.1 = f32[1,256]{1,0:T(1,128)} custom-call(bf16[128,512]{1,0:T(8,128)(2,1)} %hidden.1, bf16[2048,2048]{1,0:T(8,128)(2,1)} %head.1, s32[1,128]{1,0:T(1,128)} %bitcast.4, s32[1,128]{1,0:T(1,128)} %bitcast.5, s32[1,8]{1,0:T(1,128)} %lengths.1), custom_call_target="tpu_custom_call" | custom-call | tf_op jit(solution)/shard_map/score/pallas_call | solution.py:443
  89.3 1.1 %slice.7 = f32[1,8]{1,0:T(1,128)} slice(f32[1,256]{1,0:T(1,128)} %score.1), slice={[0:1], [128:136]} | slice | bytes 64 | tf_op jit(solution)/shard_map/slice | solution.py:477
  90.4 1.2 %slice_bitcast_fusion = f32[128]{0:T(128)} fusion(f32[1,256]{1,0:T(1,128)} %score.1), kind=kLoop, calls=%fused_computation | loop fusion | bytes 1024 | tf_op jit(solution)/shard_map/squeeze | solution.py:477
